TPU v7x, 32 devices: a whole 2x2x4 slice. The times are simulated.
32 devices in a mesh: rep: 4 (over y, core), shard: 4 (over z), ctx: 2 (over x).
Axes of the slice: x: 2, y: 2, z: 4, core: 2. Of those that a mesh axis runs over, the one named last changes fastest.
Arguments:
- tokens: bfloat16 [2, 4, 512, 2048], P(None, 'rep', ('shard', 'ctx')), may hold values from -6 to 6
- span_starts: int32 [2, 4], P(None, 'rep'), may hold values from 0 to 256
- cotangent: bfloat16 [2, 4, 512, 2048], P(None, 'rep', ('shard', 'ctx')), may hold values from -6 to 6
- w_query: bfloat16 [2048, 2048], P('shard'), may hold values from -0.125 to 0.125
- key_weight: bfloat16 [2048, 1024], P('shard'), may hold values from -0.125 to 0.125
- value_weight: bfloat16 [2048, 1024], P('shard'), may hold values from -0.125 to 0.125
- w_out: bfloat16 [2048, 2048], P('shard'), may hold values from -0.75 to 0.75
- attn_gain: bfloat16 [2048], P('shard'), may hold values from 0.099609375 to 1.8984375
- query_gain: bfloat16 [128], P('shard'), may hold values from 0.099609375 to 1.8984375
- key_gain: bfloat16 [128], P('shard'), may hold values from 0.099609375 to 1.8984375
- w_gate: bfloat16 [2048, 6144], P('shard'), may hold values from -0.125 to 0.125
- w_up: bfloat16 [2048, 6144], P('shard'), may hold values from -0.125 to 0.125
- w_down: bfloat16 [6144, 2048], P('shard'), may hold values from -0.078125 to 0.078125
- ffn_gain: bfloat16 [2048], P('shard'), may hold values from 0.099609375 to 1.8984375
Outputs:
- output: bfloat16 [2, 4, 512, 2048], P(None, 'rep', ('shard', 'ctx'))
- input_grad: float32 [2, 4, 512, 2048], P(None, 'rep', ('shard', 'ctx'))
- grad_query: float32 [2048, 2048], P('shard')
- grad_key: float32 [2048, 1024], P('shard')
- grad_value: float32 [2048, 1024], P('shard')
- grad_out: float32 [2048, 2048], P('shard')
- grad_attn_gain: float32 [2048], P('shard')
- grad_query_gain: float32 [128], P('shard')
- grad_key_gain: float32 [128], P('shard')
- grad_gate: float32 [2048, 6144], P('shard')
- grad_up: float32 [2048, 6144], P('shard')
- grad_down: float32 [6144, 2048], P('shard')
- grad_ffn_gain: float32 [2048], P('shard')
Inputs may be any that keep to these rules, and one draw needn't show every extreme that they name: `span_starts`: each sequence's picture span covers positions start to start + 255 of that sequence.
All inputs are finite; a program needn't handle non-finite values.
Results may differ from a plain program's by a relative error of at most 0.023.
Values may be sent and summed in bfloat16 or wider, within the bound.
No kernel may reach another device: no remote copies, remote signals or barrier semaphores. Data moves between devices by JAX's collectives and lax.ppermute only.
A program may use at most 448 MiB of HBM per device.

v0:
```python
from functools import partial
import jax
import jax.numpy as jnp
from jax import lax
from jax.sharding import PartitionSpec as P

QUERY_HEADS = 16
KEY_VALUE_HEADS = 8
HEAD_SIZE = 128
PIC = 256
EPSILON = 1e-06
THETA = 1000000.0


def apply_rotation(values):
    half_width = values.shape[-1] // 2
    return jnp.concatenate([-values[..., half_width:], values[..., :half_width]], axis=-1)


def rotate_back(values):
    half_width = values.shape[-1] // 2
    return jnp.concatenate([values[..., half_width:], -values[..., :half_width]], axis=-1)


def spin_tables(positions):
    inverse = THETA ** (-jnp.arange(HEAD_SIZE // 2, dtype=jnp.float32) * 2.0 / HEAD_SIZE)
    angles = positions.astype(jnp.float32)[:, None] * inverse[None, :]
    cosine_table = jnp.concatenate([jnp.cos(angles), jnp.cos(angles)], axis=-1)[:, None, :]
    sine_values = jnp.concatenate([jnp.sin(angles), jnp.sin(angles)], axis=-1)[:, None, :]
    return (cosine_table, sine_values)


def recip_rms(values):
    return lax.rsqrt(jnp.mean(values * values, axis=-1, keepdims=True) + EPSILON)


def norm_back(unit, recip, gain, d_normed):
    d_unit = d_normed * gain
    return recip * (d_unit - unit * jnp.mean(d_unit * unit, axis=-1, keepdims=True))


def over_rows(left, right):
    return lax.dot_general(
        left, right, (((0,), (0,)), ((), ())), preferred_element_type=jnp.float32
    )


def compared_to(left, right):
    return lax.dot_general(
        left, right, (((1,), (1,)), ((), ())), preferred_element_type=jnp.float32
    )


def attention_set(w_query, key_weight, value_weight, w_out, attn_gain, query_gain, key_gain):
    return (
        lax.all_gather(w_query, "shard", axis=0, tiled=True),
        lax.all_gather(key_weight, "shard", axis=0, tiled=True),
        lax.all_gather(value_weight, "shard", axis=0, tiled=True),
        lax.all_gather(w_out, "shard", axis=0, tiled=True),
        lax.all_gather(attn_gain, "shard", axis=0, tiled=True),
        lax.all_gather(query_gain, "shard", axis=0, tiled=True),
        lax.all_gather(key_gain, "shard", axis=0, tiled=True),
    )


def feedforward_set(w_gate, w_up, w_down, ffn_gain):
    return (
        lax.all_gather(w_gate, "shard", axis=0, tiled=True),
        lax.all_gather(w_up, "shard", axis=0, tiled=True),
        lax.all_gather(w_down, "shard", axis=0, tiled=True),
        lax.all_gather(ffn_gain, "shard", axis=0, tiled=True),
    )


def masked_scores(allowed, q_head, k_head):
    scores = jnp.einsum(
        "tgd,sd->gts", q_head, k_head, preferred_element_type=jnp.float32
    ) * HEAD_SIZE ** (-0.5)
    return jnp.where(allowed, scores, -1e30)


def head_forward(allowed, pieces):
    q_head, k_head, v_head = pieces
    scores = masked_scores(allowed, q_head, k_head)
    highest = jnp.max(scores, axis=-1, keepdims=True)
    log_total = highest + jnp.log(jnp.sum(jnp.exp(scores - highest), axis=-1, keepdims=True))
    probs_low = jnp.exp(scores - log_total).astype(jnp.bfloat16)
    mixed = jnp.einsum("gts,sd->tgd", probs_low, v_head, preferred_element_type=jnp.float32)
    return (mixed, log_total)


def head_backward(allowed, pieces):
    q_head, k_head, v_head, d_mix_head, log_total = pieces
    probs = jnp.exp(masked_scores(allowed, q_head, k_head) - log_total)
    probs_low = probs.astype(jnp.bfloat16)
    d_probs = jnp.einsum("tgd,sd->gts", d_mix_head, v_head, preferred_element_type=jnp.float32)
    d_values = jnp.einsum("gts,tgd->sd", probs_low, d_mix_head, preferred_element_type=jnp.float32)
    row_dot = jnp.sum(probs * d_probs, axis=-1, keepdims=True)
    d_scores = (probs * (d_probs - row_dot)).astype(jnp.bfloat16)
    d_queries = jnp.einsum(
        "gts,sd->tgd", d_scores, k_head, preferred_element_type=jnp.float32
    ) * HEAD_SIZE ** (-0.5)
    d_keys = jnp.einsum(
        "gts,tgd->sd", d_scores, q_head, preferred_element_type=jnp.float32
    ) * HEAD_SIZE ** (-0.5)
    return (d_queries, d_keys, d_values)


def shards(
    tokens,
    span_starts,
    cotangent,
    w_query,
    key_weight,
    value_weight,
    w_out,
    attn_gain,
    query_gain,
    key_gain,
    w_gate,
    w_up,
    w_down,
    ffn_gain,
):
    seq_count = lax.axis_size(("shard", "ctx"))
    seq_rank = lax.axis_index(("shard", "ctx"))
    token_rows = tokens.shape[2]
    token_length = token_rows * seq_count
    group_width = QUERY_HEADS // KEY_VALUE_HEADS
    local_pos = seq_rank * token_rows + jnp.arange(token_rows, dtype=jnp.int32)
    key_pos = jnp.arange(token_length, dtype=jnp.int32)
    cosine_table, sine_values = spin_tables(local_pos)
    cos_keys = cosine_table[:, 0, :][None]
    sin_keys = sine_values[:, 0, :][None]
    out_list = []
    grad_list = []
    stored = []
    totals = None
    for micro_index in range(tokens.shape[0]):
        span_start = span_starts[micro_index, 0]
        inside_q = (local_pos >= span_start) & (local_pos < span_start + PIC)
        inside_k = (key_pos >= span_start) & (key_pos < span_start + PIC)
        allowed = (key_pos[None, :] <= local_pos[:, None]) | inside_q[:, None] & inside_k[None, :]
        hidden_in = tokens[micro_index, 0].astype(jnp.float32)
        full_query, full_key, full_value, complete_output, gain_attn, gain_query, gain_key = (
            attention_set(w_query, key_weight, value_weight, w_out, attn_gain, query_gain, key_gain)
        )
        gain_attn = gain_attn.astype(jnp.float32)
        gain_query = gain_query.astype(jnp.float32)
        gain_key = gain_key.astype(jnp.float32)
        recip_h = recip_rms(hidden_in)
        unit_h = hidden_in * recip_h
        normalized_rows = (unit_h * gain_attn).astype(jnp.bfloat16)
        q_pre = jnp.dot(normalized_rows, full_query, preferred_element_type=jnp.float32).reshape(
            token_rows, QUERY_HEADS, HEAD_SIZE
        )
        key_before_rotation = jnp.transpose(
            jnp.dot(normalized_rows, full_key, preferred_element_type=jnp.float32).reshape(
                token_rows, KEY_VALUE_HEADS, HEAD_SIZE
            ),
            (1, 0, 2),
        )
        value_local = jnp.transpose(
            jnp.dot(normalized_rows, full_value, preferred_element_type=jnp.float32)
            .astype(jnp.bfloat16)
            .reshape(token_rows, KEY_VALUE_HEADS, HEAD_SIZE),
            (1, 0, 2),
        )
        recip_q = recip_rms(q_pre)
        unit_query = q_pre * recip_q
        recip_k = recip_rms(key_before_rotation)
        unit_k = key_before_rotation * recip_k
        scaled_q = unit_query * gain_query
        scaled_k = unit_k * gain_key
        query_rows = jnp.transpose(
            (scaled_q * cosine_table + apply_rotation(scaled_q) * sine_values)
            .astype(jnp.bfloat16)
            .reshape(token_rows, KEY_VALUE_HEADS, group_width, HEAD_SIZE),
            (1, 0, 2, 3),
        )
        key_local = (scaled_k * cos_keys + apply_rotation(scaled_k) * sin_keys).astype(jnp.bfloat16)
        key_rows, value_matrix = (
            lax.all_gather(key_local, ("shard", "ctx"), axis=1, tiled=True),
            lax.all_gather(value_local, ("shard", "ctx"), axis=1, tiled=True),
        )
        mixed_split, log_total = lax.map(
            partial(head_forward, allowed), (query_rows, key_rows, value_matrix)
        )
        mixed_heads = (
            jnp.transpose(mixed_split, (1, 0, 2, 3))
            .reshape(token_rows, QUERY_HEADS * HEAD_SIZE)
            .astype(jnp.bfloat16)
        )
        middle = hidden_in + jnp.dot(
            mixed_heads, complete_output, preferred_element_type=jnp.float32
        )
        full_gate, full_up, full_down, gain_ffn = feedforward_set(w_gate, w_up, w_down, ffn_gain)
        gain_ffn = gain_ffn.astype(jnp.float32)
        recip_m = recip_rms(middle)
        unit_m = middle * recip_m
        ffn_in = (unit_m * gain_ffn).astype(jnp.bfloat16)
        gate_pre = jnp.dot(ffn_in, full_gate, preferred_element_type=jnp.float32)
        up_pre = jnp.dot(ffn_in, full_up, preferred_element_type=jnp.float32)
        sigma = jax.nn.sigmoid(gate_pre)
        act_gate = gate_pre * sigma
        inner_act = (act_gate * up_pre).astype(jnp.bfloat16)
        result = middle + jnp.dot(inner_act, full_down, preferred_element_type=jnp.float32)
        out_list.append(result.astype(jnp.bfloat16))
        cot_rows = cotangent[micro_index, 0]
        cot_float = cot_rows.astype(jnp.float32)
        d_inner = compared_to(cot_rows, full_down)
        d_gate = (d_inner * up_pre * sigma * (1.0 + gate_pre * (1.0 - sigma))).astype(jnp.bfloat16)
        d_up = (d_inner * act_gate).astype(jnp.bfloat16)
        d_ffn_in = compared_to(d_gate, full_gate) + compared_to(d_up, full_up)
        ffn_gain_part = jnp.sum(d_ffn_in * unit_m, axis=0)
        d_middle = cot_float + norm_back(unit_m, recip_m, gain_ffn, d_ffn_in)
        branch_gradient = d_middle.astype(jnp.bfloat16)
        d_mixed = jnp.transpose(
            compared_to(branch_gradient, complete_output)
            .astype(jnp.bfloat16)
            .reshape(token_rows, KEY_VALUE_HEADS, group_width, HEAD_SIZE),
            (1, 0, 2, 3),
        )
        d_split_q, d_keys, d_values = lax.map(
            partial(head_backward, allowed),
            (query_rows, key_rows, value_matrix, d_mixed, log_total),
        )
        d_queries = jnp.transpose(d_split_q, (1, 0, 2, 3)).reshape(
            token_rows, QUERY_HEADS, HEAD_SIZE
        )
        d_key_local, d_value_local = (
            lax.psum_scatter(
                d_keys.astype(jnp.bfloat16), ("shard", "ctx"), scatter_dimension=1, tiled=True
            ).astype(jnp.float32),
            lax.psum_scatter(
                d_values.astype(jnp.bfloat16), ("shard", "ctx"), scatter_dimension=1, tiled=True
            ).astype(jnp.float32),
        )
        d_unit_q = d_queries * cosine_table + rotate_back(d_queries * sine_values)
        d_unit_k = d_key_local * cos_keys + rotate_back(d_key_local * sin_keys)
        query_gain_part = jnp.sum(d_unit_q * unit_query, axis=(0, 1))
        key_gain_part = jnp.sum(d_unit_k * unit_k, axis=(0, 1))
        d_q_pre = (
            norm_back(unit_query, recip_q, gain_query, d_unit_q)
            .astype(jnp.bfloat16)
            .reshape(token_rows, QUERY_HEADS * HEAD_SIZE)
        )
        d_k_pre = jnp.transpose(
            norm_back(unit_k, recip_k, gain_key, d_unit_k).astype(jnp.bfloat16), (1, 0, 2)
        ).reshape(token_rows, KEY_VALUE_HEADS * HEAD_SIZE)
        d_v_pre = jnp.transpose(d_value_local.astype(jnp.bfloat16), (1, 0, 2)).reshape(
            token_rows, KEY_VALUE_HEADS * HEAD_SIZE
        )
        d_normed = (
            compared_to(d_q_pre, full_query)
            + compared_to(d_k_pre, full_key)
            + compared_to(d_v_pre, full_value)
        )
        attn_gain_part = jnp.sum(d_normed * unit_h, axis=0)
        grad_list.append(d_middle + norm_back(unit_h, recip_h, gain_attn, d_normed))
        stored.append(
            (
                normalized_rows,
                d_q_pre,
                d_k_pre,
                d_v_pre,
                mixed_heads,
                branch_gradient,
                ffn_in,
                d_gate,
                d_up,
                inner_act,
                cot_rows,
            )
        )
        parts = (attn_gain_part, query_gain_part, key_gain_part, ffn_gain_part)
        if totals is None:
            totals = parts
        else:
            totals = tuple((older + newer for older, newer in zip(totals, parts)))
    joined = [
        jnp.concatenate([saved_set[member] for saved_set in stored], axis=0) for member in range(11)
    ]
    (
        normed_all,
        dq_all,
        dk_all,
        dv_all,
        mixed_all,
        branch_all,
        ffn_all,
        gate_all,
        up_all,
        inner_all,
        cot_all,
    ) = joined
    totals = (
        lax.psum_scatter(
            over_rows(normed_all, dq_all).astype(jnp.bfloat16),
            "shard",
            scatter_dimension=0,
            tiled=True,
        ).astype(jnp.float32),
        lax.psum_scatter(
            over_rows(normed_all, dk_all).astype(jnp.bfloat16),
            "shard",
            scatter_dimension=0,
            tiled=True,
        ).astype(jnp.float32),
        lax.psum_scatter(
            over_rows(normed_all, dv_all).astype(jnp.bfloat16),
            "shard",
            scatter_dimension=0,
            tiled=True,
        ).astype(jnp.float32),
        lax.psum_scatter(
            over_rows(mixed_all, branch_all).astype(jnp.bfloat16),
            "shard",
            scatter_dimension=0,
            tiled=True,
        ).astype(jnp.float32),
        lax.psum_scatter(
            totals[0].astype(jnp.bfloat16), "shard", scatter_dimension=0, tiled=True
        ).astype(jnp.float32),
        lax.psum_scatter(
            totals[1].astype(jnp.bfloat16), "shard", scatter_dimension=0, tiled=True
        ).astype(jnp.float32),
        lax.psum_scatter(
            totals[2].astype(jnp.bfloat16), "shard", scatter_dimension=0, tiled=True
        ).astype(jnp.float32),
        lax.psum_scatter(
            over_rows(ffn_all, gate_all).astype(jnp.bfloat16),
            "shard",
            scatter_dimension=0,
            tiled=True,
        ).astype(jnp.float32),
        lax.psum_scatter(
            over_rows(ffn_all, up_all).astype(jnp.bfloat16),
            "shard",
            scatter_dimension=0,
            tiled=True,
        ).astype(jnp.float32),
        lax.psum_scatter(
            over_rows(inner_all, cot_all).astype(jnp.bfloat16),
            "shard",
            scatter_dimension=0,
            tiled=True,
        ).astype(jnp.float32),
        lax.psum_scatter(
            totals[3].astype(jnp.bfloat16), "shard", scatter_dimension=0, tiled=True
        ).astype(jnp.float32),
    )
    summed = (
        lax.psum(totals[0].astype(jnp.bfloat16), ("rep", "ctx")).astype(jnp.float32),
        lax.psum(totals[1].astype(jnp.bfloat16), ("rep", "ctx")).astype(jnp.float32),
        lax.psum(totals[2].astype(jnp.bfloat16), ("rep", "ctx")).astype(jnp.float32),
        lax.psum(totals[3].astype(jnp.bfloat16), ("rep", "ctx")).astype(jnp.float32),
        lax.psum(totals[4].astype(jnp.bfloat16), ("rep", "ctx")).astype(jnp.float32),
        lax.psum(totals[5].astype(jnp.bfloat16), ("rep", "ctx")).astype(jnp.float32),
        lax.psum(totals[6].astype(jnp.bfloat16), ("rep", "ctx")).astype(jnp.float32),
        lax.psum(totals[7].astype(jnp.bfloat16), ("rep", "ctx")).astype(jnp.float32),
        lax.psum(totals[8].astype(jnp.bfloat16), ("rep", "ctx")).astype(jnp.float32),
        lax.psum(totals[9].astype(jnp.bfloat16), ("rep", "ctx")).astype(jnp.float32),
        lax.psum(totals[10].astype(jnp.bfloat16), ("rep", "ctx")).astype(jnp.float32),
    )
    output = jnp.stack(out_list)[:, None]
    input_grad = jnp.stack(grad_list)[:, None]
    return (
        output,
        input_grad,
        summed[0],
        summed[1],
        summed[2],
        summed[3],
        summed[4],
        summed[5],
        summed[6],
        summed[7],
        summed[8],
        summed[9],
        summed[10],
    )


def solution(mesh):
    in_specs = (
        P(None, "rep", ("shard", "ctx"), None),
        P(None, "rep"),
        P(None, "rep", ("shard", "ctx"), None),
        P("shard", None),
        P("shard", None),
        P("shard", None),
        P("shard", None),
        P("shard"),
        P("shard"),
        P("shard"),
        P("shard", None),
        P("shard", None),
        P("shard", None),
        P("shard"),
    )
    out_specs = (
        P(None, "rep", ("shard", "ctx"), None),
        P(None, "rep", ("shard", "ctx"), None),
        P("shard", None),
        P("shard", None),
        P("shard", None),
        P("shard", None),
        P("shard"),
        P("shard"),
        P("shard"),
        P("shard", None),
        P("shard", None),
        P("shard", None),
        P("shard"),
    )
    return jax.shard_map(shards, mesh=mesh, in_specs=in_specs, out_specs=out_specs, check_vma=False)
```

profile of v0, /device:TPU:0, one launch (start us, length us, event | category | flops | bytes accessed | tf_op | source)
XLA Modules:
  0.0 4428.3 jit_solution(448300715896860769)
XLA Ops:
  9.5 13.5 all-gather
  24.9 10.8 all-reduce.9
  36.3 57.1 %all-gather.18.cloned.1.call-done = bf16[2048,1024]{1,0:T(8,128)(2,1)} async-done(((bf16[512,1024]{1,0:T(8,128)(2,1)}), bf16[2048,1024]{1,0:T(8,128)(2,1)}) %all-gather.18.cloned.1.call-update) | async-done | bytes 4194320 | tf_op jit(solution)/shard_map/all_gather | solution.py:57
  93.4 6.4 copy.52
  99.8 4.3 multiply_reduce_fusion.18
  108.0 66.2 %all-gather.14.cloned.1.call-done = bf16[2048,1024]{1,0:T(8,128)(2,1)} async-done(((bf16[512,1024]{1,0:T(8,128)(2,1)}), bf16[2048,1024]{1,0:T(8,128)(2,1)}) %all-gather.14.cloned.1.call-update) | async-done | bytes 4194320 | tf_op jit(solution)/shard_map/all_gather | solution.py:58
  174.3 3.0 fusion.113
  178.6 3.1 fusion.114
  185.4 14.3 all-gather.1
  204.3 119.9 %all-gather.22.cloned.1.call-done = bf16[2048,2048]{1,0:T(8,128)(2,1)} async-done(((bf16[512,2048]{1,0:T(8,128)(2,1)}), bf16[2048,2048]{1,0:T(8,128)(2,1)}) %all-gather.22.cloned.1.call-update) | async-done | bytes 8388624 | tf_op jit(solution)/shard_map/all_gather | solution.py:56
  324.2 12.2 copy.53
  336.4 6.3 multiply_reduce_fusion.11
  342.8 2.8 multiply_reduce_fusion.13
  347.2 18.0 all-gather.20.cloned.1.call-done
  365.2 41.6 all-gather.16.cloned.1.call-done
  406.8 21.4 while.56
  429.4 19.0 all-gather.34.cloned.1.call-done
  448.4 41.7 all-gather.32.cloned.1.call-done
  490.2 21.6 while.57
  512.4 127.8 %all-gather.24.cloned.1.call-done = bf16[2048,2048]{1,0:T(8,128)(2,1)} async-done(((bf16[512,2048]{1,0:T(8,128)(2,1)}), bf16[2048,2048]{1,0:T(8,128)(2,1)}) %all-gather.24.cloned.1.call-update) | async-done | bytes 8388624 | tf_op jit(solution)/shard_map/all_gather | solution.py:59
  640.2 5.2 multiply_reduce_fusion.12
  647.8 417.4 %all-gather.26.cloned.1.call-done = bf16[2048,6144]{1,0:T(8,128)(2,1)} async-done(((bf16[512,6144]{1,0:T(8,128)(2,1)}), bf16[2048,6144]{1,0:T(8,128)(2,1)}) %all-gather.26.cloned.1.call-update) | async-done | bytes 25165840 | tf_op jit(solution)/shard_map/all_gather | solution.py:68
  1065.2 13.1 fusion.214
  1078.3 411.7 %all-gather.28.cloned.1.call-done = bf16[2048,6144]{1,0:T(8,128)(2,1)} async-done(((bf16[512,6144]{1,0:T(8,128)(2,1)}), bf16[2048,6144]{1,0:T(8,128)(2,1)}) %all-gather.28.cloned.1.call-update) | async-done | bytes 25165840 | tf_op jit(solution)/shard_map/all_gather | solution.py:69
  1490.0 13.4 fusion.215
  1503.4 411.6 %all-gather.30.cloned.1.call-done = bf16[6144,2048]{1,0:T(8,128)(2,1)} async-done(((bf16[1536,2048]{1,0:T(8,128)(2,1)}), bf16[6144,2048]{1,0:T(8,128)(2,1)}) %all-gather.30.cloned.1.call-update) | async-done | bytes 25165840 | tf_op jit(solution)/shard_map/all_gather | solution.py:70
  1915.0 13.7 multiply_convert_fusion.4
  1928.7 13.5 fusion.218
  1942.2 14.1 multiply_reduce_fusion.3
  1956.3 12.0 fusion.217
  1968.3 11.6 fusion.216
  1979.9 13.8 multiply_convert_fusion.2
  1993.7 13.3 fusion.219
  2007.0 14.2 multiply_reduce_fusion.2
  2024.1 6.0 convolution_convert_fusion.7
  2033.3 55.3 %while.59 = (s32[]{:T(128)}, f32[8,64,2,128]{3,1,2,0:T(8,128)S(1)}, bf16[8,512,128]{2,1,0:T(8,128)(2,1)}, bf16[8,512,128]{2,1,0:T(8,128)(2,1)}, bf16[8,512,128]{...) while((s32[]{:T(128)}, f32[8,64,2,128]{3,1,2,0:T(8,128)S(1)}, ...), condition=%wide.region_28.29_spmd.clone, body=%wide.region_26.28_spmd.clone.sunk | while | flops 84656000 | bytes 3154369 | solution.py:224
  2088.7 7.0 convolution_convert_fusion.8
  2102.3 60.2 %while.58 = (s32[]{:T(128)}, f32[8,64,2,128]{3,1,2,0:T(8,128)}, bf16[8,512,128]{2,1,0:T(8,128)(2,1)}, bf16[8,512,128]{2,1,0:T(8,128)(2,1)}, bf16[8,512,128]{2,1,...) while((s32[]{:T(128)}, f32[8,64,2,128]{3,1,2,0:T(8,128)}, ...), condition=%wide.region_19.20_spmd.clone, body=%wide.region_17.19_spmd.clone.sunk | while | flops 84656000 | bytes 3154369 | solution.py:224
  2165.4 63.3 %reduce-scatter.14.cloned.1.call-done = bf16[8,64,128]{2,1,0:T(8,128)(2,1)} async-done(((bf16[8,512,128]{2,1,0:T(8,128)(2,1)}), bf16[8,64,128]{2,1,0:T(8,128)(2,1)}) %reduce-scatter.14.cloned.1.call-update) | async-done | bytes 131088 | tf_op jit(solution)/shard_map/reduce_scatter | solution.py:235
  2229.6 4.2 convolution_convert_fusion.5
  2234.1 61.2 %reduce-scatter.16.cloned.1.call-done = bf16[8,64,128]{2,1,0:T(8,128)(2,1)} async-done(((bf16[8,512,128]{2,1,0:T(8,128)(2,1)}), bf16[8,64,128]{2,1,0:T(8,128)(2,1)}) %reduce-scatter.16.cloned.1.call-update) | async-done | bytes 131088 | tf_op jit(solution)/shard_map/reduce_scatter | solution.py:232
  2295.3 67.1 %reduce-scatter.12.cloned.1.call-done = bf16[8,64,128]{2,1,0:T(8,128)(2,1)} async-done(((bf16[8,512,128]{2,1,0:T(8,128)(2,1)}), bf16[8,64,128]{2,1,0:T(8,128)(2,1)}) %reduce-scatter.12.cloned.1.call-update) | async-done | bytes 131088 | tf_op jit(solution)/shard_map/reduce_scatter | solution.py:232
  2367.7 3.5 convolution_convert_fusion.6
  2372.2 6.8 convolution_convert_fusion.3
  2384.8 5.8 convolution_convert_fusion.4
  2391.0 13.0 convolution_convert_fusion.1
  2405.2 12.9 convolution_convert_fusion.2
  2419.3 13.0 convolution_convert_fusion
  2432.5 8.3 reduce-scatter.24.cloned.1.call-done
  2440.9 80.1 %reduce-scatter.22.cloned.1.call-done = bf16[512,1024]{1,0:T(8,128)(2,1)} async-done(((bf16[2048,1024]{1,0:T(8,128)(2,1)}), bf16[512,1024]{1,0:T(8,128)(2,1)}) %reduce-scatter.22.cloned.1.call-update) | async-done | bytes 1048592 | tf_op jit(solution)/shard_map/reduce_scatter | solution.py:304
  2521.0 147.8 %reduce-scatter.26.cloned.1.call-done = bf16[512,2048]{1,0:T(8,128)(2,1)} async-done(((bf16[2048,2048]{1,0:T(8,128)(2,1)}), bf16[512,2048]{1,0:T(8,128)(2,1)}) %reduce-scatter.26.cloned.1.call-update) | async-done | bytes 2097168 | tf_op jit(solution)/shard_map/reduce_scatter | solution.py:316
  2668.8 148.2 %reduce-scatter.20.cloned.1.call-done = bf16[512,2048]{1,0:T(8,128)(2,1)} async-done(((bf16[2048,2048]{1,0:T(8,128)(2,1)}), bf16[512,2048]{1,0:T(8,128)(2,1)}) %reduce-scatter.20.cloned.1.call-update) | async-done | bytes 2097168 | tf_op jit(solution)/shard_map/reduce_scatter | solution.py:298
  2816.9 417.4 %reduce-scatter.30.cloned.1.call-done = bf16[512,6144]{1,0:T(8,128)(2,1)} async-done(((bf16[2048,6144]{1,0:T(8,128)(2,1)}), bf16[512,6144]{1,0:T(8,128)(2,1)}) %reduce-scatter.30.cloned.1.call-update) | async-done | bytes 6291472 | tf_op jit(solution)/shard_map/reduce_scatter | solution.py:337
  3234.3 418.7 %reduce-scatter.28.cloned.1.call-done = bf16[512,6144]{1,0:T(8,128)(2,1)} async-done(((bf16[2048,6144]{1,0:T(8,128)(2,1)}), bf16[512,6144]{1,0:T(8,128)(2,1)}) %reduce-scatter.28.cloned.1.call-update) | async-done | bytes 6291472 | tf_op jit(solution)/shard_map/reduce_scatter | solution.py:331
  3653.0 418.6 %reduce-scatter.32.cloned.1.call-done = bf16[1536,2048]{1,0:T(8,128)(2,1)} async-done(((bf16[6144,2048]{1,0:T(8,128)(2,1)}), bf16[1536,2048]{1,0:T(8,128)(2,1)}) %reduce-scatter.32.cloned.1.call-update) | async-done | bytes 6291472 | tf_op jit(solution)/shard_map/reduce_scatter | solution.py:343
  4074.1 10.7 fusion.101
  4084.8 11.2 fusion.100
  4099.6 2.7 fusion.198
  4109.2 12.9 all-reduce.8
  4122.4 14.5 all-reduce.6
  4143.1 248.2 %all-reduce.12.cloned.1.call-done = (bf16[512,2048]{1,0:T(8,128)(2,1)}, bf16[512,1024]{1,0:T(8,128)(2,1)}, bf16[512,1024]{1,0:T(8,128)(2,1)}, bf16[512,2048]{1,0...) async-done(((bf16[512,2048]{1,0:T(8,128)(2,1)}, bf16[512,1024]{1,0:T(8,128)(2,1)}, bf16[512,1024]{1,0:T(8,128)(2,1)}, ...) | async-done | bytes 25165840 | tf_op jit(solution)/shard_map/psum | solution.py:354
  4391.3 9.4 convert_element_type.355
  4400.6 6.4 convert_element_type.357
  4407.0 6.3 convert_element_type.359
  (585 shorter events, 236.4 us)
Async XLA Ops:
  7.2 15.9 copy-start.89
  7.2 17.2 copy-start.102
  7.2 17.4 copy-start.103
  7.2 28.8 copy-start.5
  7.2 86.1 %all-gather.18.cloned.1.call-start = ((), (), s32[]{:S(2)}) async-start(), calls=%async_computation.13 | async-start | bytes 5242880 | tf_op jit(solution)/shard_map/all_gather | solution.py:57
  8.0 166.3 %all-gather.14.cloned.1.call-start = ((), (), s32[]{:S(2)}) async-start(), calls=%async_computation.11 | async-start | bytes 5242880 | tf_op jit(solution)/shard_map/all_gather | solution.py:58
  8.7 315.4 %all-gather.22.cloned.1.call-start = ((), (), s32[]{:S(2)}) async-start(), calls=%async_computation.15 | async-start | bytes 10485760 | tf_op jit(solution)/shard_map/all_gather | solution.py:56
  9.5 355.8 %all-gather.20.cloned.1.call-start = ((), (), s32[]{:S(2)}) async-start(), calls=%async_computation.14 | async-start | bytes 1179648 | tf_op jit(solution)/shard_map/all_gather | solution.py:183
  23.1 319.7 %copy-start.59 = (f32[4,1,512]{2,1,0:T(1,128)}, f32[4,1,512]{2,1,0:T(1,128)S(1)}, u32[]{:S(2)}) copy-start(f32[4,1,512]{2,1,0:T(1,128)S(1)} %convert_element_type.364) | copy-start | bytes 24580
  35.7 70.0 %copy-start.87 = (f32[128]{0:T(128)}, f32[128]{0:T(128)S(1)}, u32[]{:S(2)}) copy-start(f32[128]{0:T(128)S(1)} %convert_element_type.293) | copy-start | bytes 1540
  36.0 2326.4 %copy-start.58 = (f32[64,128]{1,0:T(8,128)}, f32[64,128]{1,0:T(8,128)S(1)}, u32[]{:S(2)}) copy-start(f32[64,128]{1,0:T(8,128)S(1)} %get-tuple-element.560) | copy-start | bytes 98308
  36.0 2327.7 %copy-start.56 = (f32[64,128]{1,0:T(8,128)}, f32[64,128]{1,0:T(8,128)S(1)}, u32[]{:S(2)}) copy-start(f32[64,128]{1,0:T(8,128)S(1)} %get-tuple-element.559) | copy-start | bytes 98308
  36.3 300.2 %copy-start.77 = (f32[64]{0:T(128)}, f32[64]{0:T(128)S(1)}, u32[]{:S(2)}) copy-start(f32[64]{0:T(128)S(1)} %get-tuple-element.557) | copy-start | bytes 772
  36.3 306.5 %copy-start.75 = (f32[64]{0:T(128)}, f32[64]{0:T(128)S(1)}, u32[]{:S(2)}) copy-start(f32[64]{0:T(128)S(1)} %get-tuple-element.558) | copy-start | bytes 772
  107.7 299.1 %all-gather.16.cloned.1.call-start = ((), (), s32[]{:S(2)}) async-start(), calls=%async_computation.12 | async-start | bytes 1179648 | tf_op jit(solution)/shard_map/all_gather | solution.py:184
  108.0 73.7 %copy-start.20 = (bf16[64,2048]{1,0:T(8,128)(2,1)}, bf16[64,2048]{1,0:T(8,128)(2,1)S(1)}, u32[]{:S(2)}) copy-start(bf16[64,2048]{1,0:T(8,128)(2,1)S(1)} %get-tuple-element.493) | copy-start | bytes 786436
  108.0 73.7 %copy-start.23 = (bf16[64,2048]{1,0:T(8,128)(2,1)}, bf16[64,2048]{1,0:T(8,128)(2,1)S(1)}, u32[]{:S(2)}) copy-start(bf16[64,2048]{1,0:T(8,128)(2,1)S(1)} %get-tuple-element.494) | copy-start | bytes 786436
  178.0 270.4 %all-gather.34.cloned.1.call-start = ((), (), s32[]{:S(2)}) async-start(), calls=%async_computation.21 | async-start | bytes 1179648 | tf_op jit(solution)/shard_map/all_gather | solution.py:183
  178.6 311.6 %all-gather.32.cloned.1.call-start = ((), (), s32[]{:S(2)}) async-start(), calls=%async_computation.20 | async-start | bytes 1179648 | tf_op jit(solution)/shard_map/all_gather | solution.py:184
  182.4 457.7 %all-gather.24.cloned.1.call-start = ((), (), s32[]{:S(2)}) async-start(), calls=%async_computation.16 | async-start | bytes 10485760 | tf_op jit(solution)/shard_map/all_gather | solution.py:59
  183.2 882.0 %all-gather.26.cloned.1.call-start = ((), (), s32[]{:S(2)}) async-start(), calls=%async_computation.17 | async-start | bytes 31457280 | tf_op jit(solution)/shard_map/all_gather | solution.py:68
  183.9 1306.1 %all-gather.28.cloned.1.call-start = ((), (), s32[]{:S(2)}) async-start(), calls=%async_computation.18 | async-start | bytes 31457280 | tf_op jit(solution)/shard_map/all_gather | solution.py:69
  184.5 15.2 copy-start.90
  184.5 1730.5 %all-gather.30.cloned.1.call-start = ((), (), s32[]{:S(2)}) async-start(), calls=%async_computation.19 | async-start | bytes 31457280 | tf_op jit(solution)/shard_map/all_gather | solution.py:70
  185.3 1978.6 %reduce-scatter.18.cloned.1.call-start = ((), (), s32[]{:S(2)}) async-start(), calls=%async_computation.25 | async-start | bytes 1179648 | tf_op jit(solution)/shard_map/reduce_scatter | solution.py:235
  185.4 151.0 %copy-start.44 = (bf16[8,64,2,128]{3,1,2,0:T(8,128)(2,1)}, bf16[8,64,2,128]{3,1,2,0:T(8,128)(2,1)S(1)}, u32[]{:S(2)}) copy-start(bf16[8,64,2,128]{3,1,2,0:T(8,128)(2,1)S(1)} %fusion.209) | copy-start | bytes 786436
  185.4 160.2 %copy-start.80 = (f32[128]{0:T(128)}, f32[128]{0:T(128)S(1)}, u32[]{:S(2)}) copy-start(f32[128]{0:T(128)S(1)} %convert_element_type.296) | copy-start | bytes 1540
  346.4 60.4 %copy-start.46 = (bf16[8,64,2,128]{3,1,2,0:T(8,128)(2,1)S(1)}, bf16[8,64,2,128]{3,1,2,0:T(8,128)(2,1)}, u32[]{:S(2)}) copy-start(bf16[8,64,2,128]{3,1,2,0:T(8,128)(2,1)} %copy-done.44) | copy-start | bytes 786436
  347.2 142.9 %copy-start.45 = (bf16[8,64,2,128]{3,1,2,0:T(8,128)(2,1)S(1)}, bf16[8,64,2,128]{3,1,2,0:T(8,128)(2,1)}, u32[]{:S(2)}) copy-start(bf16[8,64,2,128]{3,1,2,0:T(8,128)(2,1)} %copy-done.44) | copy-start | bytes 786436
  429.4 216.0 %copy-start.38 = (bf16[64,2048]{1,0:T(8,128)(2,1)}, bf16[64,2048]{1,0:T(8,128)(2,1)S(1)}, u32[]{:S(2)}) copy-start(bf16[64,2048]{1,0:T(8,128)(2,1)S(1)} %convert_element_type.300) | copy-start | bytes 786436
  512.4 133.0 %copy-start.40 = (bf16[64,2048]{1,0:T(8,128)(2,1)}, bf16[64,2048]{1,0:T(8,128)(2,1)S(1)}, u32[]{:S(2)}) copy-start(bf16[64,2048]{1,0:T(8,128)(2,1)S(1)} %convert_element_type.316) | copy-start | bytes 786436
  646.0 1375.3 %copy-start.85 = (f32[64]{0:T(128)}, f32[64]{0:T(128)S(1)}, u32[]{:S(2)}) copy-start(f32[64]{0:T(128)S(1)} %add_rsqrt_fusion.6) | copy-start | bytes 772
  647.7 1373.6 %copy-start.83 = (f32[64]{0:T(128)}, f32[64]{0:T(128)S(1)}, u32[]{:S(2)}) copy-start(f32[64]{0:T(128)S(1)} %add_rsqrt_fusion.4) | copy-start | bytes 772
  647.8 842.2 %copy-start.19 = (bf16[64,2048]{1,0:T(8,128)(2,1)}, bf16[64,2048]{1,0:T(8,128)(2,1)S(1)}, u32[]{:S(2)}) copy-start(bf16[64,2048]{1,0:T(8,128)(2,1)S(1)} %multiply_convert_fusion.11) | copy-start | bytes 786436
  1078.3 836.7 %copy-start.11 = (bf16[2,1,64,2048]{3,2,1,0:T(8,128)(2,1)S(1)}, bf16[2,1,64,2048]{3,2,1,0:T(8,128)(2,1)}, u32[]{:S(2)}) copy-start(bf16[2,1,64,2048]{3,2,1,0:T(8,128)(2,1)} %param.24) | copy-start | bytes 1572868
  1928.7 13.5 copy-start.10
  2099.2 129.5 %reduce-scatter.14.cloned.1.call-start = ((), (), s32[]{:S(2)}) async-start(), calls=%async_computation.23 | async-start | bytes 1179648 | tf_op jit(solution)/shard_map/reduce_scatter | solution.py:235
  2102.3 127.3 %copy-start.21 = (bf16[64,2048]{1,0:T(8,128)(2,1)S(1)}, bf16[64,2048]{1,0:T(8,128)(2,1)}, u32[]{:S(2)}) copy-start(bf16[64,2048]{1,0:T(8,128)(2,1)} %copy-done.20) | copy-start | bytes 786436
  2102.3 127.3 %copy-start.24 = (bf16[64,2048]{1,0:T(8,128)(2,1)S(1)}, bf16[64,2048]{1,0:T(8,128)(2,1)}, u32[]{:S(2)}) copy-start(bf16[64,2048]{1,0:T(8,128)(2,1)} %copy-done.23) | copy-start | bytes 786436
  2162.6 132.7 %reduce-scatter.16.cloned.1.call-start = ((), (), s32[]{:S(2)}) async-start(), calls=%async_computation.24 | async-start | bytes 1179648 | tf_op jit(solution)/shard_map/reduce_scatter | solution.py:232
  2163.2 199.2 %reduce-scatter.12.cloned.1.call-start = ((), (), s32[]{:S(2)}) async-start(), calls=%async_computation.22 | async-start | bytes 1179648 | tf_op jit(solution)/shard_map/reduce_scatter | solution.py:232
  2163.8 277.1 %reduce-scatter.24.cloned.1.call-start = ((), (), s32[]{:S(2)}) async-start(), calls=%async_computation.28 | async-start | bytes 5242880 | tf_op jit(solution)/shard_map/reduce_scatter | solution.py:310
  2233.8 129.9 %copy-start.70 = (f32[8,64]{1,0:T(8,128)S(1)}, f32[8,64]{1,0:T(8,128)}, u32[]{:S(2)}) copy-start(f32[8,64]{1,0:T(8,128)} %copy-done.69) | copy-start | bytes 6148
  2233.8 129.9 %copy-start.72 = (f32[8,64]{1,0:T(8,128)S(1)}, f32[8,64]{1,0:T(8,128)}, u32[]{:S(2)}) copy-start(f32[8,64]{1,0:T(8,128)} %copy-done.71) | copy-start | bytes 6148
  2233.8 129.9 %copy-start.88 = (f32[128]{0:T(128)S(1)}, f32[128]{0:T(128)}, u32[]{:S(2)}) copy-start(f32[128]{0:T(128)} %copy-done.87) | copy-start | bytes 1540
  2233.9 287.1 %reduce-scatter.22.cloned.1.call-start = ((), (), s32[]{:S(2)}) async-start(), calls=%async_computation.27 | async-start | bytes 5242880 | tf_op jit(solution)/shard_map/reduce_scatter | solution.py:304
  2371.2 297.6 %reduce-scatter.26.cloned.1.call-start = ((), (), s32[]{:S(2)}) async-start(), calls=%async_computation.29 | async-start | bytes 10485760 | tf_op jit(solution)/shard_map/reduce_scatter | solution.py:316
  2379.0 437.9 %reduce-scatter.20.cloned.1.call-start = ((), (), s32[]{:S(2)}) async-start(), calls=%async_computation.26 | async-start | bytes 10485760 | tf_op jit(solution)/shard_map/reduce_scatter | solution.py:298
  2390.6 843.8 %reduce-scatter.30.cloned.1.call-start = ((), (), s32[]{:S(2)}) async-start(), calls=%async_computation.31 | async-start | bytes 31457280 | tf_op jit(solution)/shard_map/reduce_scatter | solution.py:337
  2404.0 1249.0 %reduce-scatter.28.cloned.1.call-start = ((), (), s32[]{:S(2)}) async-start(), calls=%async_computation.30 | async-start | bytes 31457280 | tf_op jit(solution)/shard_map/reduce_scatter | solution.py:331
  2418.1 1653.6 %reduce-scatter.32.cloned.1.call-start = ((), (), s32[]{:S(2)}) async-start(), calls=%async_computation.32 | async-start | bytes 31457280 | tf_op jit(solution)/shard_map/reduce_scatter | solution.py:343
  2432.3 1958.9 %all-reduce.12.cloned.1.call-start = ((), (), s32[]{:S(2)}) async-start(), calls=%async_computation.33 | async-start | bytes 50331648 | tf_op jit(solution)/shard_map/psum | solution.py:354
  4074.1 10.7 copy-start.14
  4074.1 22.7 slice-start
  4084.8 12.1 slice-start.1
  4084.8 12.1 copy-start.43
  4106.7 32.4 copy-start.28
  4106.7 32.4 copy-start.84
  4106.8 32.4 copy-start.94
  4106.8 33.8 copy-start.27
  4106.8 33.8 copy-start.86
  4106.8 33.8 copy-start.92
  4391.2 9.4 copy-start.26
  4391.2 15.8 slice-start.2
  (67 other events, 177.9 us)
Sparse Core Ops, SparseCore 0:
  9.6 83.6 all-gather.17
  94.9 79.2 all-gather.13
  175.8 148.2 all-gather.21
  326.8 38.4 all-gather.19
  367.8 38.9 all-gather.15
  409.4 38.9 all-gather.33
  451.2 38.9 all-gather.31
  491.7 148.4 all-gather.23
  641.8 423.3 all-gather.25
  1066.6 423.3 all-gather.27
  1491.6 423.3 all-gather.29
  2099.3 62.1 reduce-scatter.17
  2165.9 62.7 reduce-scatter.13
  2232.5 62.7 reduce-scatter.15
  2299.5 62.8 reduce-scatter.11
  2365.1 75.7 reduce-scatter.23
  2443.7 77.2 reduce-scatter.21
  2523.8 144.9 reduce-scatter.25
  2671.7 145.1 reduce-scatter.19
  2819.2 415.1 reduce-scatter.29
  3236.8 416.1 reduce-scatter.27
  3655.4 416.1 reduce-scatter.31
  4077.4 313.7 all-reduce.11
where the time goes:
time: 4440 us; the launch traced here: 4430 us
  waiting for transfers between devices  3820 us (86%)
  matrix products  416 us (9%)
  blocking collectives  66 us (1%)
  other arithmetic  63.2 us (1%)
    reduce_scatter x1, waiting for transfers between devices, shards(): lax.psum_scatter(over_rows(ffn_all, gate_all).astype(jnp.bfloat16), 'shar...  419 us
    reduce_scatter x1, waiting for transfers between devices, shards(): lax.psum_scatter(over_rows(inner_all, cot_all).astype(jnp.bfloat16), 'sha...  419 us
    all_gather x1, waiting for transfers between devices, feedforward_set(): lax.all_gather(w_gate, 'shard', axis=0, tiled=True)  417 us
    reduce_scatter x1, waiting for transfers between devices, shards(): lax.psum_scatter(over_rows(ffn_all, up_all).astype(jnp.bfloat16), 'shard'...  417 us
    all_gather x1, waiting for transfers between devices, feedforward_set(): lax.all_gather(w_up, 'shard', axis=0, tiled=True)  412 us
    all_gather x1, waiting for transfers between devices, feedforward_set(): lax.all_gather(w_down, 'shard', axis=0, tiled=True)  412 us
    psum x1, waiting for transfers between devices, shards(): lax.psum(totals[0].astype(jnp.bfloat16), ('rep', 'ctx')).astype(jnp.float32)  248 us
    reduce_scatter x1, waiting for transfers between devices, shards(): lax.psum_scatter(over_rows(normed_all, dq_all).astype(jnp.bfloat16), 'sha...  148 us
  transfers between devices with their start and end apart: 23, of which 22 were waited for; matrix products, arithmetic and copies ran while one was open for 7% of the time, Pallas kernels for 0%

commit v1 on v0

--- a/solution.py
+++ b/solution.py
@@ -10,6 +10,27 @@
 PIC = 256
 EPSILON = 1e-06
 THETA = 1000000.0
+
+
+def joined_along(pieces, dim):
+    shape = list(pieces.shape[1:])
+    shape[dim] *= pieces.shape[0]
+    return jnp.moveaxis(pieces, 0, dim).reshape(shape)
+
+
+def grow_blocks(value, axis):
+    size, here = (lax.axis_size(axis), lax.axis_index(axis))
+    parts, bit = (value[None], 1)
+    while bit < size:
+        other = lax.ppermute(parts, axis, [(i, i ^ bit) for i in range(size)])
+        low = here & bit == 0
+        parts = jnp.concatenate([jnp.where(low, parts, other), jnp.where(low, other, parts)])
+        bit *= 2
+    return parts
+
+
+def collect(x, axis, dim):
+    return joined_along(grow_blocks(x, axis), dim)
 
 
 def apply_rotation(values):
@@ -67,7 +88,7 @@
     return (
         lax.all_gather(w_gate, "shard", axis=0, tiled=True),
         lax.all_gather(w_up, "shard", axis=0, tiled=True),
-        lax.all_gather(w_down, "shard", axis=0, tiled=True),
+        collect(w_down, "shard", 0),
         lax.all_gather(ffn_gain, "shard", axis=0, tiled=True),
     )
 

time: 4440 us -> 4690 us (1.056)
  blocking collectives: 66 us -> 331 us
  waiting for transfers between devices: 3820 us -> 3750 us
  other arithmetic: 63.2 us -> 112 us
    all_gather x1 -> x0, waiting for transfers between devices: 412 us -> none  [feedforward_set(): lax.all_gather(w_down, 'shard', axis=0, tiled=True)]
    all_gather x1, blocking collectives: 14.3 us -> 278 us  [feedforward_set(): lax.all_gather(ffn_gain, 'shard', axis=0, tiled=True)]
    all_gather x2, waiting for transfers between devices: 83.3 us -> 347 us  [shards(): lax.all_gather(value_local, ('shard', 'ctx'), axis=1, tiled=True)]
    all_gather x2, waiting for transfers between devices: 37 us -> 279 us  [shards(): lax.all_gather(key_local, ('shard', 'ctx'), axis=1, tiled=True)]
    all_gather x1, waiting for transfers between devices: 120 us -> 0.01 us  [attention_set(): lax.all_gather(w_query, 'shard', axis=0, tiled=True)]
  transfers between devices with their start and end apart: 23 -> 24, of which waited for: 22 -> 20; matrix products, arithmetic and copies ran while one was open for 7% -> 7% of each run, Pallas kernels for 0% -> 0%
where the time goes in v1:
time: 4690 us; the launch traced here: 4670 us
  waiting for transfers between devices  3750 us (80%)
  matrix products  409 us (9%)
  blocking collectives  331 us (7%)
  other arithmetic  112 us (2%)
  local copies, waits for them, and re-layouts  50.9 us (1%)
    reduce_scatter x1, waiting for transfers between devices, shards(): lax.psum_scatter(over_rows(ffn_all, gate_all).astype(jnp.bfloat16), 'shar...  419 us
    reduce_scatter x1, waiting for transfers between devices, shards(): lax.psum_scatter(over_rows(ffn_all, up_all).astype(jnp.bfloat16), 'shard'...  419 us
    reduce_scatter x1, waiting for transfers between devices, shards(): lax.psum_scatter(over_rows(inner_all, cot_all).astype(jnp.bfloat16), 'sha...  418 us
    all_gather x1, waiting for transfers between devices, feedforward_set(): lax.all_gather(w_up, 'shard', axis=0, tiled=True)  411 us
    all_gather x1, waiting for transfers between devices, feedforward_set(): lax.all_gather(w_gate, 'shard', axis=0, tiled=True)  378 us
    all_gather x2, waiting for transfers between devices, shards(): lax.all_gather(value_local, ('shard', 'ctx'), axis=1, tiled=True)  347 us
    all_gather x2, waiting for transfers between devices, shards(): lax.all_gather(key_local, ('shard', 'ctx'), axis=1, tiled=True)  279 us
    all_gather x1, blocking collectives, feedforward_set(): lax.all_gather(ffn_gain, 'shard', axis=0, tiled=True)  278 us
  transfers between devices with their start and end apart: 24, of which 20 were waited for; matrix products, arithmetic and copies ran while one was open for 7% of the time, Pallas kernels for 0%

profile of v1, /device:TPU:0, one launch (start us, length us, event | category | flops | bytes accessed | tf_op | source)
XLA Modules:
  0.0 4674.9 jit_solution(12912534979594036416)
XLA Ops:
  10.2 13.5 all-gather
  27.4 11.5 all-reduce.9
  40.6 52.7 %all-gather.17.cloned.1.call-done = bf16[2048,1024]{1,0:T(8,128)(2,1)} async-done(((bf16[512,1024]{1,0:T(8,128)(2,1)}), bf16[2048,1024]{1,0:T(8,128)(2,1)}) %all-gather.17.cloned.1.call-update) | async-done | bytes 4194320 | tf_op jit(solution)/shard_map/all_gather | solution.py:78
  93.3 6.4 copy.52
  99.7 4.1 multiply_reduce_fusion.18
  103.9 3.8 multiply_reduce_fusion.19
  109.9 64.3 %all-gather.13.cloned.1.call-done = bf16[2048,1024]{1,0:T(8,128)(2,1)} async-done(((bf16[512,1024]{1,0:T(8,128)(2,1)}), bf16[2048,1024]{1,0:T(8,128)(2,1)}) %all-gather.13.cloned.1.call-update) | async-done | bytes 4194320 | tf_op jit(solution)/shard_map/all_gather | solution.py:79
  178.6 3.1 fusion.114
  184.7 278.4 %all-gather.1 = bf16[4,1,512]{2,1,0:T(2,128)(2,1)S(1)} all-gather(bf16[1,1,512]{2,1,0:T(2,128)(2,1)S(1)} %reshape.361), channel_id=1, replica_groups=mesh['rep'=4,'shard'=4,'ctx'=2] {'shard'}, dimensions={0}, use_global_device_ids=true | all-gather | bytes 5120 | tf_op jit(solution)/shard_map/all_gather | solution.py:92
  467.7 5.3 broadcast_select_fusion.3
  473.0 6.8 pad_maximum_fusion.1
  482.5 12.3 copy.53
  494.8 6.3 multiply_reduce_fusion.11
  505.4 259.9 %all-gather.19.cloned.1.call-done = bf16[8,512,128]{2,1,0:T(8,128)(2,1)} async-done(((bf16[8,64,128]{2,1,0:T(8,128)(2,1)}), bf16[8,512,128]{2,1,0:T(8,128)(2,1)}) %all-gather.19.cloned.1.call-update) | async-done | bytes 1048592 | tf_op jit(solution)/shard_map/all_gather | solution.py:204
  765.3 305.5 %all-gather.15.cloned.1.call-done = bf16[8,512,128]{2,1,0:T(8,128)(2,1)} async-done(((bf16[8,64,128]{2,1,0:T(8,128)(2,1)}), bf16[8,512,128]{2,1,0:T(8,128)(2,1)}) %all-gather.15.cloned.1.call-update) | async-done | bytes 1048592 | tf_op jit(solution)/shard_map/all_gather | solution.py:205
  1070.8 21.4 while.56
  1093.5 18.9 all-gather.31.cloned.1.call-done
  1112.4 41.7 all-gather.29.cloned.1.call-done
  1154.2 21.6 while.57
  1176.4 127.7 %all-gather.23.cloned.1.call-done = bf16[2048,2048]{1,0:T(8,128)(2,1)} async-done(((bf16[512,2048]{1,0:T(8,128)(2,1)}), bf16[2048,2048]{1,0:T(8,128)(2,1)}) %all-gather.23.cloned.1.call-update) | async-done | bytes 8388624 | tf_op jit(solution)/shard_map/all_gather | solution.py:80
  1304.1 5.2 multiply_reduce_fusion.12
  1316.1 14.6 broadcast_select_fusion.1
  1330.7 20.5 pad_maximum_fusion
  1351.2 378.0 %all-gather.25.cloned.1.call-done = bf16[2048,6144]{1,0:T(8,128)(2,1)} async-done(((bf16[512,6144]{1,0:T(8,128)(2,1)}), bf16[2048,6144]{1,0:T(8,128)(2,1)}) %all-gather.25.cloned.1.call-update) | async-done | bytes 25165840 | tf_op jit(solution)/shard_map/all_gather | solution.py:89
  1729.2 13.6 fusion.212
  1742.8 411.2 %all-gather.27.cloned.1.call-done = bf16[2048,6144]{1,0:T(8,128)(2,1)} async-done(((bf16[512,6144]{1,0:T(8,128)(2,1)}), bf16[2048,6144]{1,0:T(8,128)(2,1)}) %all-gather.27.cloned.1.call-update) | async-done | bytes 25165840 | tf_op jit(solution)/shard_map/all_gather | solution.py:90
  2154.0 10.6 fusion.213
  2164.6 17.3 multiply_convert_fusion.4
  2181.9 13.7 fusion.216
  2195.5 13.4 multiply_reduce_fusion.3
  2208.9 10.7 fusion.215
  2219.6 10.7 fusion.214
  2230.3 17.0 multiply_convert_fusion.2
  2247.3 13.8 fusion.217
  2261.1 14.5 multiply_reduce_fusion.2
  2277.3 6.2 convolution_convert_fusion.7
  2285.8 50.2 %while.59 = (s32[]{:T(128)}, f32[8,64,2,128]{3,1,2,0:T(8,128)S(1)}, bf16[8,512,128]{2,1,0:T(8,128)(2,1)S(1)}, bf16[8,512,128]{2,1,0:T(8,128)(2,1)}, bf16[8,512,1...) while((s32[]{:T(128)}, f32[8,64,2,128]{3,1,2,0:T(8,128)S(1)}, ...), condition=%wide.region_28.29_spmd.clone, body=%wide.region_26.28_spmd.clone.sunk | while | flops 84656000 | bytes 3154369 | solution.py:245
  2336.0 7.3 convolution_convert_fusion.8
  2347.6 60.5 %while.58 = (s32[]{:T(128)}, f32[8,64,2,128]{3,1,2,0:T(8,128)S(1)}, bf16[8,512,128]{2,1,0:T(8,128)(2,1)}, bf16[8,512,128]{2,1,0:T(8,128)(2,1)}, bf16[8,512,128]{...) while((s32[]{:T(128)}, f32[8,64,2,128]{3,1,2,0:T(8,128)S(1)}, ...), condition=%wide.region_19.20_spmd.clone, body=%wide.region_17.19_spmd.clone.sunk | while | flops 84656000 | bytes 3154369 | solution.py:245
  2410.5 64.2 %reduce-scatter.14.cloned.1.call-done = bf16[8,64,128]{2,1,0:T(8,128)(2,1)} async-done(((bf16[8,512,128]{2,1,0:T(8,128)(2,1)}), bf16[8,64,128]{2,1,0:T(8,128)(2,1)}) %reduce-scatter.14.cloned.1.call-update) | async-done | bytes 131088 | tf_op jit(solution)/shard_map/reduce_scatter | solution.py:256
  2475.7 3.3 convolution_convert_fusion.5
  2479.1 62.4 %reduce-scatter.16.cloned.1.call-done = bf16[8,64,128]{2,1,0:T(8,128)(2,1)} async-done(((bf16[8,512,128]{2,1,0:T(8,128)(2,1)}), bf16[8,64,128]{2,1,0:T(8,128)(2,1)}) %reduce-scatter.16.cloned.1.call-update) | async-done | bytes 131088 | tf_op jit(solution)/shard_map/reduce_scatter | solution.py:253
  2541.5 67.1 %reduce-scatter.12.cloned.1.call-done = bf16[8,64,128]{2,1,0:T(8,128)(2,1)} async-done(((bf16[8,512,128]{2,1,0:T(8,128)(2,1)}), bf16[8,64,128]{2,1,0:T(8,128)(2,1)}) %reduce-scatter.12.cloned.1.call-update) | async-done | bytes 131088 | tf_op jit(solution)/shard_map/reduce_scatter | solution.py:253
  2613.2 3.3 convolution_convert_fusion.6
  2616.8 5.8 convolution_convert_fusion.3
  2629.6 5.8 convolution_convert_fusion.4
  2637.2 13.2 convolution_convert_fusion
  2650.4 13.4 convolution_convert_fusion.1
  2663.9 13.3 convolution_convert_fusion.2
  2677.4 9.6 reduce-scatter.24.cloned.1.call-done
  2687.1 80.1 %reduce-scatter.22.cloned.1.call-done = bf16[512,1024]{1,0:T(8,128)(2,1)} async-done(((bf16[2048,1024]{1,0:T(8,128)(2,1)}), bf16[512,1024]{1,0:T(8,128)(2,1)}) %reduce-scatter.22.cloned.1.call-update) | async-done | bytes 1048592 | tf_op jit(solution)/shard_map/reduce_scatter | solution.py:325
  2767.2 147.8 %reduce-scatter.26.cloned.1.call-done = bf16[512,2048]{1,0:T(8,128)(2,1)} async-done(((bf16[2048,2048]{1,0:T(8,128)(2,1)}), bf16[512,2048]{1,0:T(8,128)(2,1)}) %reduce-scatter.26.cloned.1.call-update) | async-done | bytes 2097168 | tf_op jit(solution)/shard_map/reduce_scatter | solution.py:337
  2915.0 148.0 %reduce-scatter.20.cloned.1.call-done = bf16[512,2048]{1,0:T(8,128)(2,1)} async-done(((bf16[2048,2048]{1,0:T(8,128)(2,1)}), bf16[512,2048]{1,0:T(8,128)(2,1)}) %reduce-scatter.20.cloned.1.call-update) | async-done | bytes 2097168 | tf_op jit(solution)/shard_map/reduce_scatter | solution.py:319
  3063.0 417.5 %reduce-scatter.32.cloned.1.call-done = bf16[1536,2048]{1,0:T(8,128)(2,1)} async-done(((bf16[6144,2048]{1,0:T(8,128)(2,1)}), bf16[1536,2048]{1,0:T(8,128)(2,1)}) %reduce-scatter.32.cloned.1.call-update) | async-done | bytes 6291472 | tf_op jit(solution)/shard_map/reduce_scatter | solution.py:364
  3480.5 418.5 %reduce-scatter.30.cloned.1.call-done = bf16[512,6144]{1,0:T(8,128)(2,1)} async-done(((bf16[2048,6144]{1,0:T(8,128)(2,1)}), bf16[512,6144]{1,0:T(8,128)(2,1)}) %reduce-scatter.30.cloned.1.call-update) | async-done | bytes 6291472 | tf_op jit(solution)/shard_map/reduce_scatter | solution.py:358
  3899.1 418.6 %reduce-scatter.28.cloned.1.call-done = bf16[512,6144]{1,0:T(8,128)(2,1)} async-done(((bf16[2048,6144]{1,0:T(8,128)(2,1)}), bf16[512,6144]{1,0:T(8,128)(2,1)}) %reduce-scatter.28.cloned.1.call-update) | async-done | bytes 6291472 | tf_op jit(solution)/shard_map/reduce_scatter | solution.py:352
  4320.2 10.7 fusion.101
  4330.9 11.2 fusion.100
  4355.3 12.9 all-reduce.8
  4368.6 14.5 all-reduce.6
  4389.2 248.1 %all-reduce.12.cloned.1.call-done = (bf16[512,2048]{1,0:T(8,128)(2,1)}, bf16[512,1024]{1,0:T(8,128)(2,1)}, bf16[512,1024]{1,0:T(8,128)(2,1)}, bf16[512,2048]{1,0...) async-done(((bf16[512,2048]{1,0:T(8,128)(2,1)}, bf16[512,1024]{1,0:T(8,128)(2,1)}, bf16[512,1024]{1,0:T(8,128)(2,1)}, ...) | async-done | bytes 25165840 | tf_op jit(solution)/shard_map/psum | solution.py:375
  4637.3 9.4 convert_element_type.355
  4646.7 6.4 convert_element_type.357
  4653.1 6.3 convert_element_type.359
  (612 shorter events, 241.5 us)
Async XLA Ops:
  7.2 86.1 %all-gather.17.cloned.1.call-start = ((), (), s32[]{:S(2)}) async-start(), calls=%async_computation.13 | async-start | bytes 5242880 | tf_op jit(solution)/shard_map/all_gather | solution.py:78
  7.9 91.8 %copy-start.6 = (bf16[2,1,64,2048]{3,2,1,0:T(8,128)(2,1)S(1)}, bf16[2,1,64,2048]{3,2,1,0:T(8,128)(2,1)}, u32[]{:S(2)}) copy-start(bf16[2,1,64,2048]{3,2,1,0:T(8,128)(2,1)} %param.22) | copy-start | bytes 1572868
  7.9 166.3 %all-gather.13.cloned.1.call-start = ((), (), s32[]{:S(2)}) async-start(), calls=%async_computation.11 | async-start | bytes 5242880 | tf_op jit(solution)/shard_map/all_gather | solution.py:79
  8.7 473.8 %all-gather.21.cloned.1.call-start = ((), (), s32[]{:S(2)}) async-start(), calls=%async_computation.15 | async-start | bytes 10485760 | tf_op jit(solution)/shard_map/all_gather | solution.py:77
  9.4 755.9 %all-gather.19.cloned.1.call-start = ((), (), s32[]{:S(2)}) async-start(), calls=%async_computation.14 | async-start | bytes 1179648 | tf_op jit(solution)/shard_map/all_gather | solution.py:204
  23.7 477.4 %copy-start.64 = (f32[4,1,512]{2,1,0:T(1,128)}, f32[4,1,512]{2,1,0:T(1,128)S(1)}, u32[]{:S(2)}) copy-start(f32[4,1,512]{2,1,0:T(1,128)S(1)} %convert_element_type.364) | copy-start | bytes 24580
  38.9 68.8 %copy-start.97 = (f32[128]{0:T(128)}, f32[128]{0:T(128)S(1)}, u32[]{:S(2)}) copy-start(f32[128]{0:T(128)S(1)} %convert_element_type.293) | copy-start | bytes 1540
  39.3 465.7 %copy-start.60 = (f32[64,128]{1,0:T(8,128)}, f32[64,128]{1,0:T(8,128)S(1)}, u32[]{:S(2)}) copy-start(f32[64,128]{1,0:T(8,128)S(1)} %get-tuple-element.563) | copy-start | bytes 98308
  39.3 465.7 %copy-start.62 = (f32[64,128]{1,0:T(8,128)}, f32[64,128]{1,0:T(8,128)S(1)}, u32[]{:S(2)}) copy-start(f32[64,128]{1,0:T(8,128)S(1)} %get-tuple-element.564) | copy-start | bytes 98308
  40.6 454.2 %copy-start.87 = (f32[64]{0:T(128)}, f32[64]{0:T(128)S(1)}, u32[]{:S(2)}) copy-start(f32[64]{0:T(128)S(1)} %get-tuple-element.561) | copy-start | bytes 772
  40.6 460.6 %copy-start.85 = (f32[64]{0:T(128)}, f32[64]{0:T(128)S(1)}, u32[]{:S(2)}) copy-start(f32[64]{0:T(128)S(1)} %get-tuple-element.562) | copy-start | bytes 772
  103.9 70.3 %copy-start.74 = (f32[8,64]{1,0:T(8,128)}, f32[8,64]{1,0:T(8,128)S(1)}, u32[]{:S(2)}) copy-start(f32[8,64]{1,0:T(8,128)S(1)} %add_rsqrt_fusion.2) | copy-start | bytes 6148
  107.7 66.5 %copy-start.76 = (f32[8,64]{1,0:T(8,128)}, f32[8,64]{1,0:T(8,128)S(1)}, u32[]{:S(2)}) copy-start(f32[8,64]{1,0:T(8,128)S(1)} %add_rsqrt_fusion.3) | copy-start | bytes 6148
  109.6 961.2 %all-gather.15.cloned.1.call-start = ((), (), s32[]{:S(2)}) async-start(), calls=%async_computation.12 | async-start | bytes 1179648 | tf_op jit(solution)/shard_map/all_gather | solution.py:205
  109.8 74.0 %copy-start.12 = (bf16[64,2048]{1,0:T(8,128)(2,1)}, bf16[64,2048]{1,0:T(8,128)(2,1)S(1)}, u32[]{:S(2)}) copy-start(bf16[64,2048]{1,0:T(8,128)(2,1)S(1)} %get-tuple-element.497) | copy-start | bytes 786436
  109.8 74.0 %copy-start.14 = (bf16[64,2048]{1,0:T(8,128)(2,1)}, bf16[64,2048]{1,0:T(8,128)(2,1)S(1)}, u32[]{:S(2)}) copy-start(bf16[64,2048]{1,0:T(8,128)(2,1)S(1)} %get-tuple-element.498) | copy-start | bytes 786436
  177.9 934.5 %all-gather.31.cloned.1.call-start = ((), (), s32[]{:S(2)}) async-start(), calls=%async_computation.20 | async-start | bytes 1179648 | tf_op jit(solution)/shard_map/all_gather | solution.py:204
  178.5 975.6 %all-gather.29.cloned.1.call-start = ((), (), s32[]{:S(2)}) async-start(), calls=%async_computation.19 | async-start | bytes 1179648 | tf_op jit(solution)/shard_map/all_gather | solution.py:205
  182.4 1121.8 %all-gather.23.cloned.1.call-start = ((), (), s32[]{:S(2)}) async-start(), calls=%async_computation.16 | async-start | bytes 10485760 | tf_op jit(solution)/shard_map/all_gather | solution.py:80
  183.1 280.0 %copy-start.99 = (s32[2,1]{0,1:T(1,128)S(1)}, s32[2,1]{0,1:T(1,128)}, u32[]{:S(2)}) copy-start(s32[2,1]{0,1:T(1,128)} %param.23) | copy-start | bytes 28
  183.1 1546.0 %all-gather.25.cloned.1.call-start = ((), (), s32[]{:S(2)}) async-start(), calls=%async_computation.17 | async-start | bytes 31457280 | tf_op jit(solution)/shard_map/all_gather | solution.py:89
  183.9 1970.1 %all-gather.27.cloned.1.call-start = ((), (), s32[]{:S(2)}) async-start(), calls=%async_computation.18 | async-start | bytes 31457280 | tf_op jit(solution)/shard_map/all_gather | solution.py:90
  184.5 2225.1 %reduce-scatter.18.cloned.1.call-start = ((), (), s32[]{:S(2)}) async-start(), calls=%async_computation.24 | async-start | bytes 1179648 | tf_op jit(solution)/shard_map/reduce_scatter | solution.py:256
  184.5 283.1 %collective-permute-start = (bf16[1,1536,2048]{2,1,0:T(8,128)(2,1)}, bf16[1,1536,2048]{2,1,0:T(8,128)(2,1)}, u32[]{:S(2)}, u32[]{:S(2)}) collective-permute-start(bf16[1,1536,2048]{2,1,0:T(8,128)(2,1)} %bitcast.558), channel_id=1, source_target_pairs={{0,2},{2,0},{4,6},{6,4},{1,3},{3,1},{5,7},{7,5},{8,10},{10,8},{12,... | collective-permute-start | bytes 18874376 | tf_op jit(solution)/shard_map/ppermute | solution.py:25
  184.7 288.3 %copy-start.44 = (bf16[8,64,2,128]{3,1,2,0:T(8,128)(2,1)}, bf16[8,64,2,128]{3,1,2,0:T(8,128)(2,1)S(1)}, u32[]{:S(2)}) copy-start(bf16[8,64,2,128]{3,1,2,0:T(8,128)(2,1)S(1)} %fusion.207) | copy-start | bytes 786436
  184.7 319.3 %copy-start.90 = (f32[128]{0:T(128)}, f32[128]{0:T(128)S(1)}, u32[]{:S(2)}) copy-start(f32[128]{0:T(128)S(1)} %convert_element_type.296) | copy-start | bytes 1540
  481.5 830.3 %collective-permute-start.1 = (bf16[2,1536,2048]{2,1,0:T(8,128)(2,1)}, bf16[2,1536,2048]{2,1,0:T(8,128)(2,1)}, u32[]{:S(2)}, u32[]{:S(2)}) collective-permute-start(bf16[2,1536,2048]{2,1,0:T(8,128)(2,1)} %pad_maximum_fusion.1), channel_id=1, source_target_pairs={{0,4},{2,6},{4,0},{6,2},{1,5},{3,7},{5,1},{7,3},{8,12},{10,14},{12... | collective-permute-start | bytes 37748744 | tf_op jit(solution)/shard_map/ppermute | solution.py:25
  504.0 566.8 %copy-start.46 = (bf16[8,64,2,128]{3,1,2,0:T(8,128)(2,1)S(1)}, bf16[8,64,2,128]{3,1,2,0:T(8,128)(2,1)}, u32[]{:S(2)}) copy-start(bf16[8,64,2,128]{3,1,2,0:T(8,128)(2,1)} %copy-done.44) | copy-start | bytes 786436
  504.0 566.8 %copy-start.70 = (f32[64,16]{0,1:T(8,128)}, f32[64,16]{0,1:T(8,128)S(1)}, u32[]{:S(2)}) copy-start(f32[64,16]{0,1:T(8,128)S(1)} %add_rsqrt_fusion.1) | copy-start | bytes 12292
  504.8 649.4 %copy-start.45 = (bf16[8,64,2,128]{3,1,2,0:T(8,128)(2,1)S(1)}, bf16[8,64,2,128]{3,1,2,0:T(8,128)(2,1)}, u32[]{:S(2)}) copy-start(bf16[8,64,2,128]{3,1,2,0:T(8,128)(2,1)} %copy-done.44) | copy-start | bytes 786436
  1092.3 217.1 %copy-start.78 = (pred[64]{0:T(512)(128)(4,1)}, pred[64]{0:T(512)(128)(4,1)S(1)}, u32[]{:S(2)}) copy-start(pred[64]{0:T(512)(128)(4,1)S(1)} %get-tuple-element.1107) | copy-start | bytes 196
  1092.3 217.1 %copy-start.80 = (pred[512]{0:T(512)(128)(4,1)}, pred[512]{0:T(512)(128)(4,1)S(1)}, u32[]{:S(2)}) copy-start(pred[512]{0:T(512)(128)(4,1)S(1)} %get-tuple-element.1109) | copy-start | bytes 1540
  1092.3 217.1 %copy-start.84 = (f32[8,2,64,1]{2,1,3,0:T(2,128)}, f32[8,2,64,1]{2,1,3,0:T(2,128)S(1)}, u32[]{:S(2)}) copy-start(f32[8,2,64,1]{2,1,3,0:T(2,128)S(1)} %get-tuple-element.911) | copy-start | bytes 12292
  1093.5 215.9 %copy-start.38 = (bf16[64,2048]{1,0:T(8,128)(2,1)}, bf16[64,2048]{1,0:T(8,128)(2,1)S(1)}, u32[]{:S(2)}) copy-start(bf16[64,2048]{1,0:T(8,128)(2,1)S(1)} %convert_element_type.300) | copy-start | bytes 786436
  1176.4 133.0 %copy-start.40 = (bf16[64,2048]{1,0:T(8,128)(2,1)}, bf16[64,2048]{1,0:T(8,128)(2,1)S(1)}, u32[]{:S(2)}) copy-start(bf16[64,2048]{1,0:T(8,128)(2,1)S(1)} %convert_element_type.316) | copy-start | bytes 786436
  1309.9 965.8 %copy-start.95 = (f32[64]{0:T(128)}, f32[64]{0:T(128)S(1)}, u32[]{:S(2)}) copy-start(f32[64]{0:T(128)S(1)} %add_rsqrt_fusion.6) | copy-start | bytes 772
  1311.6 964.0 %copy-start.93 = (f32[64]{0:T(128)}, f32[64]{0:T(128)S(1)}, u32[]{:S(2)}) copy-start(f32[64]{0:T(128)S(1)} %add_rsqrt_fusion.4) | copy-start | bytes 772
  1742.8 421.8 %copy-start.24 = (bf16[2,1,64,2048]{3,2,1,0:T(8,128)(2,1)S(1)}, bf16[2,1,64,2048]{3,2,1,0:T(8,128)(2,1)}, u32[]{:S(2)}) copy-start(bf16[2,1,64,2048]{3,2,1,0:T(8,128)(2,1)} %param.24) | copy-start | bytes 1572868
  2208.9 66.8 %copy-start.21 = (f32[64,2048]{1,0:T(8,128)}, f32[64,2048]{1,0:T(8,128)S(1)}, u32[]{:S(2)}) copy-start(f32[64,2048]{1,0:T(8,128)S(1)} %get-tuple-element.558) | copy-start | bytes 1572868
  2277.3 58.7 %copy-start.47 = (bf16[64,2048]{1,0:T(8,128)(2,1)}, bf16[64,2048]{1,0:T(8,128)(2,1)S(1)}, u32[]{:S(2)}) copy-start(bf16[64,2048]{1,0:T(8,128)(2,1)S(1)} %get-tuple-element.495) | copy-start | bytes 786436
  2345.2 129.5 %reduce-scatter.14.cloned.1.call-start = ((), (), s32[]{:S(2)}) async-start(), calls=%async_computation.22 | async-start | bytes 1179648 | tf_op jit(solution)/shard_map/reduce_scatter | solution.py:256
  2347.6 128.1 %copy-start.13 = (bf16[64,2048]{1,0:T(8,128)(2,1)S(1)}, bf16[64,2048]{1,0:T(8,128)(2,1)}, u32[]{:S(2)}) copy-start(bf16[64,2048]{1,0:T(8,128)(2,1)} %copy-done.12) | copy-start | bytes 786436
  2347.6 128.1 %copy-start.15 = (bf16[64,2048]{1,0:T(8,128)(2,1)S(1)}, bf16[64,2048]{1,0:T(8,128)(2,1)}, u32[]{:S(2)}) copy-start(bf16[64,2048]{1,0:T(8,128)(2,1)} %copy-done.14) | copy-start | bytes 786436
  2408.2 70.9 %copy-start.28 = (f32[8,64,2,128]{3,1,2,0:T(8,128)}, f32[8,64,2,128]{3,1,2,0:T(8,128)S(1)}, u32[]{:S(2)}) copy-start(f32[8,64,2,128]{3,1,2,0:T(8,128)S(1)} %get-tuple-element.200) | copy-start | bytes 1572868
  2408.2 133.3 %reduce-scatter.16.cloned.1.call-start = ((), (), s32[]{:S(2)}) async-start(), calls=%async_computation.23 | async-start | bytes 1179648 | tf_op jit(solution)/shard_map/reduce_scatter | solution.py:253
  2408.9 199.7 %reduce-scatter.12.cloned.1.call-start = ((), (), s32[]{:S(2)}) async-start(), calls=%async_computation.21 | async-start | bytes 1179648 | tf_op jit(solution)/shard_map/reduce_scatter | solution.py:253
  2409.5 277.6 %reduce-scatter.24.cloned.1.call-start = ((), (), s32[]{:S(2)}) async-start(), calls=%async_computation.27 | async-start | bytes 5242880 | tf_op jit(solution)/shard_map/reduce_scatter | solution.py:331
  2475.7 133.0 %copy-start.63 = (f32[64,128]{1,0:T(8,128)S(1)}, f32[64,128]{1,0:T(8,128)}, u32[]{:S(2)}) copy-start(f32[64,128]{1,0:T(8,128)} %copy-done.62) | copy-start | bytes 98308
  2475.7 134.3 %copy-start.32 = (f32[8,64,128]{2,1,0:T(8,128)S(1)}, f32[8,64,128]{2,1,0:T(8,128)}, u32[]{:S(2)}) copy-start(f32[8,64,128]{2,1,0:T(8,128)} %copy-done.31) | copy-start | bytes 786436
  2475.7 134.3 %copy-start.34 = (f32[8,64,128]{2,1,0:T(8,128)S(1)}, f32[8,64,128]{2,1,0:T(8,128)}, u32[]{:S(2)}) copy-start(f32[8,64,128]{2,1,0:T(8,128)} %copy-done.33) | copy-start | bytes 786436
  2475.7 134.3 %copy-start.61 = (f32[64,128]{1,0:T(8,128)S(1)}, f32[64,128]{1,0:T(8,128)}, u32[]{:S(2)}) copy-start(f32[64,128]{1,0:T(8,128)} %copy-done.60) | copy-start | bytes 98308
  2475.7 134.3 %copy-start.75 = (f32[8,64]{1,0:T(8,128)S(1)}, f32[8,64]{1,0:T(8,128)}, u32[]{:S(2)}) copy-start(f32[8,64]{1,0:T(8,128)} %copy-done.74) | copy-start | bytes 6148
  2475.7 134.3 %copy-start.77 = (f32[8,64]{1,0:T(8,128)S(1)}, f32[8,64]{1,0:T(8,128)}, u32[]{:S(2)}) copy-start(f32[8,64]{1,0:T(8,128)} %copy-done.76) | copy-start | bytes 6148
  2475.7 134.3 %copy-start.98 = (f32[128]{0:T(128)S(1)}, f32[128]{0:T(128)}, u32[]{:S(2)}) copy-start(f32[128]{0:T(128)} %copy-done.97) | copy-start | bytes 1540
  2479.1 288.2 %reduce-scatter.22.cloned.1.call-start = ((), (), s32[]{:S(2)}) async-start(), calls=%async_computation.26 | async-start | bytes 5242880 | tf_op jit(solution)/shard_map/reduce_scatter | solution.py:325
  2616.5 298.5 %reduce-scatter.26.cloned.1.call-start = ((), (), s32[]{:S(2)}) async-start(), calls=%async_computation.28 | async-start | bytes 10485760 | tf_op jit(solution)/shard_map/reduce_scatter | solution.py:337
  2622.6 440.4 %reduce-scatter.20.cloned.1.call-start = ((), (), s32[]{:S(2)}) async-start(), calls=%async_computation.25 | async-start | bytes 10485760 | tf_op jit(solution)/shard_map/reduce_scatter | solution.py:319
  2635.4 845.1 %reduce-scatter.32.cloned.1.call-start = ((), (), s32[]{:S(2)}) async-start(), calls=%async_computation.31 | async-start | bytes 31457280 | tf_op jit(solution)/shard_map/reduce_scatter | solution.py:364
  2650.4 1248.7 %reduce-scatter.30.cloned.1.call-start = ((), (), s32[]{:S(2)}) async-start(), calls=%async_computation.30 | async-start | bytes 31457280 | tf_op jit(solution)/shard_map/reduce_scatter | solution.py:358
  2663.8 1653.9 %reduce-scatter.28.cloned.1.call-start = ((), (), s32[]{:S(2)}) async-start(), calls=%async_computation.29 | async-start | bytes 31457280 | tf_op jit(solution)/shard_map/reduce_scatter | solution.py:352
  2677.2 1960.1 %all-reduce.12.cloned.1.call-start = ((), (), s32[]{:S(2)}) async-start(), calls=%async_computation.32 | async-start | bytes 50331648 | tf_op jit(solution)/shard_map/psum | solution.py:375
  4351.4 35.3 copy-start.22
  4351.4 35.3 copy-start.96
  4351.4 35.3 copy-start.101
  (78 other events, 547.7 us)
Sparse Core Ops, SparseCore 0:
  9.6 83.6 all-gather.16
  94.9 79.2 all-gather.12
  175.8 277.5 all-gather.20
  456.0 309.2 all-gather.18
  767.9 302.8 all-gather.14
  1073.4 38.9 all-gather.30
  1115.2 38.9 all-gather.28
  1155.7 148.3 all-gather.22
  1305.7 423.3 all-gather.24
  1730.6 423.3 all-gather.26
  2345.4 62.1 reduce-scatter.17
  2411.8 62.8 reduce-scatter.13
  2478.7 62.7 reduce-scatter.15
  2545.7 62.8 reduce-scatter.11
  2611.4 75.6 reduce-scatter.23
  2689.9 77.2 reduce-scatter.21
  2770.0 144.9 reduce-scatter.25
  2917.8 145.1 reduce-scatter.19
  3065.4 415.0 reduce-scatter.31
  3482.9 416.1 reduce-scatter.29
  3901.4 416.1 reduce-scatter.27
  4323.5 313.7 all-reduce.11
